TPU v7x, 32 devices: a whole 2x2x4 slice. The times are simulated.
32 devices in a mesh: vert: 32 (over z, y, x, core).
Axes of the slice: x: 2, y: 2, z: 4, core: 2. Of those that a mesh axis runs over, the one named last changes fastest.
Arguments:
- features: bfloat16 [32768, 512], P('vert'), may hold values from -6 to 6
- send_rows: int32 [32, 32, 4], P('vert'), may hold values from 0 to 1023
- mirror_count: int32 [32, 32], P('vert'), may hold values from 1 to 4, as said below
- tile_coord: int32 [32, 2, 128], P('vert'), may hold values from 0 to 8
- tile_mask: int32 [32, 128, 128, 128], P('vert'), may hold values 0 or 1
- tile_count: int32 [32], P('vert'), may hold values from 32 to 128, as said below
- w_self1: bfloat16 [512, 512], replicated, may hold values from -0.25 to 0.25
- w_neigh1: bfloat16 [512, 512], replicated, may hold values from -1 to 1
- bias1: bfloat16 [512], replicated, may hold values from -3 to 3
- w_self2: bfloat16 [512, 512], replicated, may hold values from -0.25 to 0.25
- w_neigh2: bfloat16 [512, 512], replicated, may hold values from -1 to 1
- bias2: bfloat16 [512], replicated, may hold values from -3 to 3
Outputs:
- embedding: bfloat16 [32768, 512], P('vert')
Inputs may be any that keep to these rules, and one draw needn't show every extreme that they name: `mirror_count`: some device has all 4 slots live on every peer, and some device receives 4 live rows from every device. `tile_count`: some device has all 128 tiles live.
All inputs are finite; a program needn't handle non-finite values. No bound on the sum of `tile_mask` on one device may be relied on, other than what follows from the above.
Results may differ from a plain program's by a relative error of at most 0.0051.
Values may be sent and summed in bfloat16 or wider, within the bound.
A program may use at most 128 MiB of HBM per device.

v0:
```python
import jax
import jax.numpy as jnp
from jax import lax
from jax.sharding import PartitionSpec as P

TGROUP = 32


def for_sending(array):

    def short(part):
        return part.astype(jnp.bfloat16) if part.dtype == jnp.float32 else part

    return jax.tree.map(short, array)


def mirror_route(parts, forward):
    if forward:
        return jax.tree.map(
            lambda part, own: part.astype(own.dtype),
            lax.all_to_all(for_sending(parts), "vert", split_axis=0, concat_axis=0, tiled=True),
            parts,
        )
    return jax.tree.map(
        lambda part, own: part.astype(own.dtype),
        lax.all_to_all(for_sending(parts), "vert", split_axis=0, concat_axis=0, tiled=True),
        parts,
    )


def aggregate(table_blocks, source_live, coords, masks, live_tiles):
    n_blocks, block, width = table_blocks.shape

    def visit(index, carry):
        totals, degree = carry
        start = index * TGROUP
        target = lax.dynamic_slice_in_dim(coords[0], start, TGROUP)
        source = lax.dynamic_slice_in_dim(coords[1], start, TGROUP)
        picked = lax.dynamic_slice_in_dim(masks, start, TGROUP, 0)
        used = start + jnp.arange(TGROUP, dtype=jnp.int32) < live_tiles
        weights = (
            jnp.where(used[:, None, None], picked, 0).astype(jnp.bfloat16)
            * jnp.take(source_live, source, axis=0)[:, None, :]
        )
        products = jnp.einsum(
            "tij,tjf->tif",
            weights,
            jnp.take(table_blocks, source, axis=0),
            preferred_element_type=jnp.float32,
        )
        totals = totals.at[target].add(products)
        degree = degree.at[target].add(jnp.sum(weights.astype(jnp.float32), axis=2))
        return (totals, degree)

    rounds = (live_tiles + TGROUP - 1) // TGROUP
    start_state = (
        jnp.zeros((n_blocks, block, width), jnp.float32),
        jnp.zeros((n_blocks, block), jnp.float32),
    )
    return lax.fori_loop(0, rounds, visit, start_state)


def body(
    features,
    send_rows,
    mirror_count,
    tile_coord,
    tile_mask,
    tile_count,
    w_self1,
    w_neigh1,
    bias1,
    w_self2,
    w_neigh2,
    bias2,
):
    number = lax.axis_size("vert")
    own_rows, width = features.shape
    slots = send_rows.shape[2]
    block = tile_mask.shape[2]
    rows_list = send_rows[0]
    flat_rows = rows_list.reshape(-1)
    live_slots = jnp.arange(slots, dtype=jnp.int32)[None, :] < mirror_count[0][:, None]
    coords = tile_coord[0]
    masks = tile_mask[0]
    live_tiles = tile_count[0]
    current = features
    source_live = None
    degree = None
    for layer, (w_self, w_neigh, bias) in enumerate(
        ((w_self1, w_neigh1, bias1), (w_self2, w_neigh2, bias2))
    ):
        outgoing = jnp.take(current, flat_rows, axis=0).reshape(number, slots, width)
        if layer == 0:
            arrived, arrived_live = mirror_route((outgoing, live_slots.astype(jnp.bfloat16)), True)
            source_live = jnp.concatenate(
                [jnp.ones((own_rows,), jnp.bfloat16), arrived_live.reshape(-1)]
            ).reshape(-1, block)
        else:
            (arrived,) = mirror_route((outgoing,), True)
        table_blocks = jnp.concatenate(
            [current, arrived.reshape(number * slots, width)], axis=0
        ).reshape(-1, block, width)
        totals, counted = aggregate(table_blocks, source_live, coords, masks, live_tiles)
        totals = totals.reshape(-1, width)
        counted = counted.reshape(-1)
        mirror_part = totals[own_rows:].reshape(number, slots, width)
        if layer == 0:
            returned = mirror_route((mirror_part, counted[own_rows:].reshape(number, slots)), False)
            degree = (
                counted[:own_rows]
                .at[flat_rows]
                .add(jnp.where(live_slots, returned[1], 0.0).reshape(-1))
            )
        else:
            returned = mirror_route((mirror_part,), False)
        summed = (
            totals[:own_rows]
            .at[flat_rows]
            .add(jnp.where(live_slots[:, :, None], returned[0], 0.0).reshape(-1, width))
        )
        mean = ((summed + current.astype(jnp.float32)) / (degree + 1.0)[:, None]).astype(
            jnp.bfloat16
        )
        pre = (
            jnp.dot(current, w_self, preferred_element_type=jnp.float32)
            + jnp.dot(mean, w_neigh, preferred_element_type=jnp.float32)
            + bias.astype(jnp.float32)
        )
        if layer == 0:
            current = jax.nn.relu(pre).astype(jnp.bfloat16)
        else:
            current = pre.astype(jnp.bfloat16)
    return current


def solution(mesh):
    in_specs = (
        P("vert", None),
        P("vert", None, None),
        P("vert", None),
        P("vert", None, None),
        P("vert", None, None, None),
        P("vert"),
        P(),
        P(),
        P(),
        P(),
        P(),
        P(),
    )
    out_specs = P("vert", None)
    return jax.shard_map(body, mesh=mesh, in_specs=in_specs, out_specs=out_specs, check_vma=False)
```

profile of v0, /device:TPU:0, one launch (start us, length us, event | category | flops | bytes accessed | tf_op | source)
XLA Modules:
  0.0 304.7 jit_solution(10062020128072646263)
XLA Ops:
  0.0 1.5 compare_convert_fusion
  1.5 7.3 %all-to-all-start = ((bf16[32,1,4]{2,1,0:T(2,128)(2,1)}), bf16[32,1,4]{2,1,0:T(2,128)(2,1)S(1)}, u32[]{:S(2)}, u32[]{:S(2)}) async-start(bf16[32,1,4]{2,1,0:T(2,128)(2,1)} %compare_convert_fusion), calls=%async_computation | async-start | bytes 32768 | tf_op jit(solution)/shard_map/all_to_all | solution.py:21
  9.5 0.8 copy.17
  10.4 0.7 iota_compare_fusion
  11.2 2.2 gather_fusion.4
  14.4 2.1 fusion.28
  17.0 5.8 %all-to-all-start.1 = ((bf16[32,4,512]{2,1,0:T(4,128)(2,1)}), bf16[32,4,512]{2,1,0:T(4,128)(2,1)S(1)}, u32[]{:S(2)}, u32[]{:S(2)}) async-start(bf16[32,4,512]{2,1,0:T(4,128)(2,1)} %reshape.258), calls=%async_computation.1 | async-start | bytes 262144 | tf_op jit(solution)/shard_map/all_to_all | solution.py:21
  23.1 8.0 %all-to-all-done.1 = bf16[32,4,512]{2,1,0:T(4,128)(2,1)S(1)} async-done(((bf16[32,4,512]{2,1,0:T(4,128)(2,1)}), bf16[32,4,512]{2,1,0:T(4,128)(2,1)S(1)}, u32[]{:S(2)}, u32[]{:S(2)}) %all-to-all-start.1) | async-done | bytes 131104 | tf_op jit(solution)/shard_map/all_to_all | solution.py:21
  31.1 1.1 pad_maximum_fusion
  32.5 55.5 %while.24 = (s32[]{:T(128)}, f32[9,128,512]{2,1,0:T(8,128)S(1)}, f32[9,128]{1,0:T(8,128)S(1)}, s32[]{:T(128)}, s32[2,128]{1,0:T(2,128)S(1)}, /*index=5*/s32[]{:T...) while((s32[]{:T(128)}, f32[9,128,512]{2,1,0:T(8,128)S(1)}, ...), condition=%wide.region_4.8_spmd, body=%wide.region_0.7_spmd.sunk | while | flops 545265024 | bytes 50454020 | solution.py:60
  32.6 0.7 compare_and_fusion.5
  34.0 4.1 %gather_fusion = bf16[32,128,512]{2,1,0:T(8,128)(2,1)} fusion(bf16[9,128,512]{2,1,0:T(8,128)(2,1)} %get-tuple-element.329, s32[1024]{0:T(1024)S(1)} %pad_clamp_fusion.5), kind=kCustom, calls=%fused_computation.2.clone.clone.1 | custom fusion | bytes 8388736 | tf_op jit(solution)/shard_map/while/body/jit(_take)/gather | solution.py:48
  38.0 7.4 %fusion.50 = f32[32,128,512]{2,1,0:T(8,128)} fusion(bf16[32,128,512]{2,1,0:T(8,128)(2,1)} %gather_fusion, pred[32]{0:T(512)(128)(4,1)S(1)} %get-tuple-element.280, s32[128,128,128]{2,1,0:T(8,128)} %get-tuple-element.327, s32[]{:T(128)S(6)} %select_n.168, pred[32]{0:T(512)(128)(4,1)S(1)} %get-tuple-element.281, ...), kind=kOutput, calls=%fused_computation.12.clone.1 | convolution fusion | flops 540540928 | bytes 14688324 | tf_op jit(solution)/shard_map/while/body/tij,tjf->tif/dot_general | solution.py:45
  45.5 11.8 %scatter_fusion = f32[9,128,512]{2,1,0:T(8,128)S(1)} fusion(f32[9,128,512]{2,1,0:T(8,128)S(1)} %get-tuple-element.309, s32[32]{0:T(128)S(1)} %fusion.49, f32[32,128,512]{2,1,0:T(8,128)} %fusion.50), kind=kCustom, calls=%fused_computation.6.clone.1 | custom fusion | flops 2097152 | bytes 25165952 | tf_op jit(solution)/shard_map/while/body/scatter-add | solution.py:51
  57.3 2.3 convert_reduce_fusion.3
  60.3 0.7 compare_and_fusion.5
  61.7 4.1 %gather_fusion = bf16[32,128,512]{2,1,0:T(8,128)(2,1)} fusion(bf16[9,128,512]{2,1,0:T(8,128)(2,1)} %get-tuple-element.329, s32[1024]{0:T(1024)S(1)} %pad_clamp_fusion.5), kind=kCustom, calls=%fused_computation.2.clone.clone.1 | custom fusion | bytes 8388736 | tf_op jit(solution)/shard_map/while/body/jit(_take)/gather | solution.py:48
  65.8 7.4 %fusion.50 = f32[32,128,512]{2,1,0:T(8,128)} fusion(bf16[32,128,512]{2,1,0:T(8,128)(2,1)} %gather_fusion, pred[32]{0:T(512)(128)(4,1)S(1)} %get-tuple-element.280, s32[128,128,128]{2,1,0:T(8,128)} %get-tuple-element.327, s32[]{:T(128)S(6)} %select_n.168, pred[32]{0:T(512)(128)(4,1)S(1)} %get-tuple-element.281, ...), kind=kOutput, calls=%fused_computation.12.clone.1 | convolution fusion | flops 540540928 | bytes 14688324 | tf_op jit(solution)/shard_map/while/body/tij,tjf->tif/dot_general | solution.py:45
  73.2 11.8 %scatter_fusion = f32[9,128,512]{2,1,0:T(8,128)S(1)} fusion(f32[9,128,512]{2,1,0:T(8,128)S(1)} %get-tuple-element.309, s32[32]{0:T(128)S(1)} %fusion.49, f32[32,128,512]{2,1,0:T(8,128)} %fusion.50), kind=kCustom, calls=%fused_computation.6.clone.1 | custom fusion | flops 2097152 | bytes 25165952 | tf_op jit(solution)/shard_map/while/body/scatter-add | solution.py:51
  85.0 2.3 convert_reduce_fusion.3
  88.2 1.0 copy-done.2
  89.3 1.7 bitcast_add_fusion.1
  91.7 56.9 %all-to-all-start.3 = ((bf16[32,1,4]{2,1,0:T(2,128)(2,1)}), bf16[32,1,4]{2,1,0:T(2,128)(2,1)S(1)}, u32[]{:S(2)}, u32[]{:S(2)}) async-start(bf16[32,1,4]{2,1,0:T(2,128)(2,1)} %convert_element_type.94), calls=%async_computation.3 | async-start | bytes 32768 | tf_op jit(solution)/shard_map/all_to_all | solution.py:26
  149.3 6.4 %all-to-all-done.3 = bf16[32,1,4]{2,1,0:T(2,128)(2,1)S(1)} async-done(((bf16[32,1,4]{2,1,0:T(2,128)(2,1)}), bf16[32,1,4]{2,1,0:T(2,128)(2,1)S(1)}, u32[]{:S(2)}, u32[]{:S(2)}) %all-to-all-start.3) | async-done | bytes 288 | tf_op jit(solution)/shard_map/all_to_all | solution.py:26
  155.7 2.6 all-to-all-start.2
  158.5 1.4 scatter_fusion.4
  159.9 6.6 %all-to-all-done.2 = bf16[32,4,512]{2,1,0:T(4,128)(2,1)S(1)} async-done(((bf16[32,4,512]{2,1,0:T(4,128)(2,1)}), bf16[32,4,512]{2,1,0:T(4,128)(2,1)S(1)}, u32[]{:S(2)}, u32[]{:S(2)}) %all-to-all-start.2) | async-done | bytes 131104 | tf_op jit(solution)/shard_map/all_to_all | solution.py:26
  166.7 4.3 %scatter_fusion.3 = f32[1024,512]{1,0:T(8,128)} fusion(f32[1024,512]{1,0:T(8,128)} %bitcast_add_fusion.1, s32[128]{0:T(128)S(1)} %fusion.24, f32[128,512]{1,0:T(8,128)S(1)} %reshape.344), kind=kCustom, calls=%fused_computation.9 | custom fusion | flops 65536 | bytes 786944 | tf_op jit(solution)/shard_map/scatter-add | solution.py:120
  171.0 3.0 maximum_convert_fusion
  174.0 0.8 gather_fusion.5
  175.7 2.6 all-to-all-start.4
  178.2 2.1 fusion.29
  180.3 6.1 %all-to-all-done.4 = bf16[32,4,512]{2,1,0:T(4,128)(2,1)S(1)} async-done(((bf16[32,4,512]{2,1,0:T(4,128)(2,1)}), bf16[32,4,512]{2,1,0:T(4,128)(2,1)S(1)}, u32[]{:S(2)}, u32[]{:S(2)}) %all-to-all-start.4) | async-done | bytes 131104 | tf_op jit(solution)/shard_map/all_to_all | solution.py:21
  186.5 1.1 pad_maximum_fusion.1
  187.9 49.6 %while.25 = (s32[]{:T(128)}, f32[9,128,512]{2,1,0:T(8,128)S(1)}, s32[]{:T(128)}, s32[2,128]{1,0:T(2,128)S(1)}, s32[]{:T(128)}, /*index=5*/s32[128,128,128]{2,1,0...) while((s32[]{:T(128)}, f32[9,128,512]{2,1,0:T(8,128)S(1)}, ...), condition=%wide.region_9.13_spmd, body=%wide.region_7.12_spmd.sunk | while | flops 542643584 | bytes 48282968 | solution.py:60
  188.1 0.7 compare_and_fusion.6
  189.5 4.1 %gather_fusion.2 = bf16[32,128,512]{2,1,0:T(8,128)(2,1)} fusion(bf16[9,128,512]{2,1,0:T(8,128)(2,1)} %get-tuple-element.365, s32[1024]{0:T(1024)S(1)} %pad_clamp_fusion.6), kind=kCustom, calls=%fused_computation.5.clone.clone.1 | custom fusion | bytes 8388736 | tf_op jit(solution)/shard_map/while/body/jit(_take)/gather | solution.py:48
  193.6 7.4 %fusion.55 = f32[32,128,512]{2,1,0:T(8,128)} fusion(bf16[32,128,512]{2,1,0:T(8,128)(2,1)} %gather_fusion.2, pred[32]{0:T(512)(128)(4,1)S(1)} %get-tuple-element.293, s32[128,128,128]{2,1,0:T(8,128)} %get-tuple-element.363, s32[]{:T(128)S(6)} %select_n.173, pred[32]{0:T(512)(128)(4,1)S(1)} %get-tuple-element.294, ...), kind=kOutput, calls=%fused_computation.31.clone.1 | convolution fusion | flops 540540928 | bytes 14688324 | tf_op jit(solution)/shard_map/while/body/tij,tjf->tif/dot_general | solution.py:45
  201.0 11.8 %scatter_fusion.2 = f32[9,128,512]{2,1,0:T(8,128)S(1)} fusion(f32[9,128,512]{2,1,0:T(8,128)S(1)} %get-tuple-element.347, s32[32]{0:T(128)S(1)} %fusion.54, f32[32,128,512]{2,1,0:T(8,128)} %fusion.55), kind=kCustom, calls=%fused_computation.8.clone.1 | custom fusion | flops 2097152 | bytes 25165952 | tf_op jit(solution)/shard_map/while/body/scatter-add | solution.py:51
  214.3 4.1 %gather_fusion.2 = bf16[32,128,512]{2,1,0:T(8,128)(2,1)} fusion(bf16[9,128,512]{2,1,0:T(8,128)(2,1)} %get-tuple-element.365, s32[1024]{0:T(1024)S(1)} %pad_clamp_fusion.6), kind=kCustom, calls=%fused_computation.5.clone.clone.1 | custom fusion | bytes 8388736 | tf_op jit(solution)/shard_map/while/body/jit(_take)/gather | solution.py:48
  218.3 7.4 %fusion.55 = f32[32,128,512]{2,1,0:T(8,128)} fusion(bf16[32,128,512]{2,1,0:T(8,128)(2,1)} %gather_fusion.2, pred[32]{0:T(512)(128)(4,1)S(1)} %get-tuple-element.293, s32[128,128,128]{2,1,0:T(8,128)} %get-tuple-element.363, s32[]{:T(128)S(6)} %select_n.173, pred[32]{0:T(512)(128)(4,1)S(1)} %get-tuple-element.294, ...), kind=kOutput, calls=%fused_computation.31.clone.1 | convolution fusion | flops 540540928 | bytes 14688324 | tf_op jit(solution)/shard_map/while/body/tij,tjf->tif/dot_general | solution.py:45
  225.8 11.8 %scatter_fusion.2 = f32[9,128,512]{2,1,0:T(8,128)S(1)} fusion(f32[9,128,512]{2,1,0:T(8,128)S(1)} %get-tuple-element.347, s32[32]{0:T(128)S(1)} %fusion.54, f32[32,128,512]{2,1,0:T(8,128)} %fusion.55), kind=kCustom, calls=%fused_computation.8.clone.1 | custom fusion | flops 2097152 | bytes 25165952 | tf_op jit(solution)/shard_map/while/body/scatter-add | solution.py:51
  237.5 1.6 slice.50
  239.9 50.7 %all-to-all-start.5 = ((bf16[32,4,512]{2,1,0:T(4,128)(2,1)}), bf16[32,4,512]{2,1,0:T(4,128)(2,1)S(1)}, u32[]{:S(2)}, u32[]{:S(2)}) async-start(bf16[32,4,512]{2,1,0:T(4,128)(2,1)} %convert_element_type.88), calls=%async_computation.5 | async-start | bytes 262144 | tf_op jit(solution)/shard_map/all_to_all | solution.py:26
  290.6 2.2 bitcast_add_fusion
  292.8 6.0 %all-to-all-done.5 = bf16[32,4,512]{2,1,0:T(4,128)(2,1)S(1)} async-done(((bf16[32,4,512]{2,1,0:T(4,128)(2,1)}), bf16[32,4,512]{2,1,0:T(4,128)(2,1)S(1)}, u32[]{:S(2)}, u32[]{:S(2)}) %all-to-all-start.5) | async-done | bytes 131104 | tf_op jit(solution)/shard_map/all_to_all | solution.py:26
  299.0 2.1 scatter_fusion.5
  301.2 3.5 %add_convert_fusion = bf16[1024,512]{1,0:T(8,128)(2,1)} fusion(f32[1024,512]{1,0:T(8,128)} %fusion.29, bf16[512,512]{1,0:T(8,128)(2,1)} %param.32, f32[512]{0:T(512)S(1)} %copy-done.6, f32[1024,512]{1,0:T(8,128)S(1)} %scatter_fusion.5, f32[1024]{0:T(1024)S(1)} %scatter_fusion.4), kind=kOutput, calls=%fused_computation.55 | convolution fusion | flops 539492352 | bytes 5773312 | tf_op jit(solution)/shard_map/dot_general | solution.py:127
  (79 shorter events, 11.4 us)
Async XLA Ops:
  0.0 14.4 %copy-start = (bf16[512,512]{1,0:T(8,128)(2,1)S(1)}, bf16[512,512]{1,0:T(8,128)(2,1)}, u32[]{:S(2)}) copy-start(bf16[512,512]{1,0:T(8,128)(2,1)} %param.28) | copy-start | bytes 1572868
  0.0 14.4 %copy-start.1 = (bf16[1024,512]{1,0:T(8,128)(2,1)S(1)}, bf16[1024,512]{1,0:T(8,128)(2,1)}, u32[]{:S(2)}) copy-start(bf16[1024,512]{1,0:T(8,128)(2,1)} %param.22) | copy-start | bytes 3145732
  1.5 15.5 %all-to-all-start = ((bf16[32,1,4]{2,1,0:T(2,128)(2,1)}), bf16[32,1,4]{2,1,0:T(2,128)(2,1)S(1)}, u32[]{:S(2)}, u32[]{:S(2)}) async-start(bf16[32,1,4]{2,1,0:T(2,128)(2,1)} %compare_convert_fusion), calls=%async_computation | async-start | bytes 32768 | tf_op jit(solution)/shard_map/all_to_all | solution.py:21
  13.5 3.0 copy-start.7
  13.5 3.0 copy-start.8
  17.0 14.0 %all-to-all-start.1 = ((bf16[32,4,512]{2,1,0:T(4,128)(2,1)}), bf16[32,4,512]{2,1,0:T(4,128)(2,1)S(1)}, u32[]{:S(2)}, u32[]{:S(2)}) async-start(bf16[32,4,512]{2,1,0:T(4,128)(2,1)} %reshape.258), calls=%async_computation.1 | async-start | bytes 262144 | tf_op jit(solution)/shard_map/all_to_all | solution.py:21
  31.1 1.4 copy-start.5
  88.0 1.2 copy-start.2
  91.7 64.0 %all-to-all-start.3 = ((bf16[32,1,4]{2,1,0:T(2,128)(2,1)}), bf16[32,1,4]{2,1,0:T(2,128)(2,1)S(1)}, u32[]{:S(2)}, u32[]{:S(2)}) async-start(bf16[32,1,4]{2,1,0:T(2,128)(2,1)} %convert_element_type.94), calls=%async_computation.3 | async-start | bytes 32768 | tf_op jit(solution)/shard_map/all_to_all | solution.py:26
  155.7 10.8 %all-to-all-start.2 = ((bf16[32,4,512]{2,1,0:T(4,128)(2,1)}), bf16[32,4,512]{2,1,0:T(4,128)(2,1)S(1)}, u32[]{:S(2)}, u32[]{:S(2)}) async-start(bf16[32,4,512]{2,1,0:T(4,128)(2,1)} %convert_element_type.79), calls=%async_computation.2 | async-start | bytes 262144 | tf_op jit(solution)/shard_map/all_to_all | solution.py:26
  166.7 4.3 %copy-start.9 = (bf16[512,512]{1,0:T(8,128)(2,1)S(1)}, bf16[512,512]{1,0:T(8,128)(2,1)}, u32[]{:S(2)}) copy-start(bf16[512,512]{1,0:T(8,128)(2,1)} %param.29) | copy-start | bytes 1572868
  174.0 12.5 %copy-start.3 = (bf16[1024,512]{1,0:T(8,128)(2,1)}, bf16[1024,512]{1,0:T(8,128)(2,1)S(1)}, u32[]{:S(2)}) copy-start(bf16[1024,512]{1,0:T(8,128)(2,1)S(1)} %maximum_convert_fusion) | copy-start | bytes 3145732
  174.0 4.2 %copy-start.4 = (bf16[512,512]{1,0:T(8,128)(2,1)S(1)}, bf16[512,512]{1,0:T(8,128)(2,1)}, u32[]{:S(2)}) copy-start(bf16[512,512]{1,0:T(8,128)(2,1)} %param.31) | copy-start | bytes 1572868
  175.7 10.8 %all-to-all-start.4 = ((bf16[32,4,512]{2,1,0:T(4,128)(2,1)}), bf16[32,4,512]{2,1,0:T(4,128)(2,1)S(1)}, u32[]{:S(2)}, u32[]{:S(2)}) async-start(bf16[32,4,512]{2,1,0:T(4,128)(2,1)} %reshape.263), calls=%async_computation.4 | async-start | bytes 262144 | tf_op jit(solution)/shard_map/all_to_all | solution.py:21
  239.9 58.9 %all-to-all-start.5 = ((bf16[32,4,512]{2,1,0:T(4,128)(2,1)}), bf16[32,4,512]{2,1,0:T(4,128)(2,1)S(1)}, u32[]{:S(2)}, u32[]{:S(2)}) async-start(bf16[32,4,512]{2,1,0:T(4,128)(2,1)} %convert_element_type.88), calls=%async_computation.5 | async-start | bytes 262144 | tf_op jit(solution)/shard_map/all_to_all | solution.py:26
  299.0 2.1 copy-start.6
where the time goes:
time: 307 us; the launch traced here: 305 us
  starting transfers between devices  126 us (41%)
  other arithmetic  73.8 us (24%)
  matrix products  40.1 us (13%)
  waiting for transfers between devices  33.2 us (11%)
  local copies, waits for them, and re-layouts  30.3 us (10%)
    all_to_all x6, starting transfers between devices, mirror_route(): lax.all_to_all(for_sending(parts), 'vert', split_axis=0, concat_axis=0, t...  126 us
    scatter-add x4, other arithmetic, visit(): totals = totals.at[target].add(products)  47.1 us
    all_to_all x6, waiting for transfers between devices, mirror_route(): lax.all_to_all(for_sending(parts), 'vert', split_axis=0, concat_axis=0, t...  33.2 us
    dot_general x4, matrix products, visit(): jnp.einsum('tij,tjf->tif', weights, jnp.take(table_blocks, source, axis=0...  29.4 us
    gather x4, local copies, waits for them, and re-layouts, visit(): jnp.take(table_blocks, source, axis=0)  16.2 us
    dot_general x2, matrix products, body(): jnp.dot(mean, w_neigh, preferred_element_type=jnp.float32)  6.51 us
    scatter-add x2, other arithmetic, body(): summed = totals[:own_rows].at[flat_rows].add(jnp.where(live_slots[:, :, N...  6.4 us
  transfers between devices with their start and end apart: 6, of which 5 were waited for; matrix products, arithmetic and copies ran while one was open for 5% of the time, Pallas kernels for 0%

commit v1 on v0

v1 whole, which is shorter than its diff:
```python
import functools

import jax
import jax.numpy as jnp
from jax import lax
from jax.experimental import pallas as pl
from jax.experimental.pallas import tpu as pltpu
from jax.sharding import PartitionSpec as P

LANES = 128
DEAD = 64.0
BF = jnp.bfloat16
F32 = jnp.float32


def mm(a, b):
    return jnp.dot(a, b, preferred_element_type=F32)


def count_kernel(group, coord, count, mask, out, held, sems):
    tiles, block, _ = mask.shape
    size = out.shape[0]
    live = count[0]
    groups = tiles // group

    def copy(g):
        span = pl.ds(g * group, group)
        return pltpu.make_async_copy(mask.at[span], held.at[span], sems.at[g])

    for g in range(groups):

        @pl.when(g * group < live)
        def _():
            copy(g).start()

    step = block

    @pl.loop(0, size // step)
    def _(b):
        rows = lax.broadcasted_iota(jnp.int32, (step, size), 0) + b * step
        cols = lax.broadcasted_iota(jnp.int32, (step, size), 1)
        out[pl.ds(pl.multiple_of(b * step, step), step), :] = jnp.where(rows == cols, 1.0, 0.0).astype(BF)

    for g in range(groups):

        @pl.when(g * group < live)
        def _():
            copy(g).wait()

            @pl.loop(g * group, jnp.minimum((g + 1) * group, live))
            def _(t):
                rows = pl.ds(pl.multiple_of(coord[0, t] * block, block), block)
                cols = pl.ds(pl.multiple_of(coord[1, t] * block, block), block)
                out[rows, cols] += held[t].astype(F32).astype(BF)


def count_edges(coord, count, mask, size):
    tiles, block, _ = mask.shape
    group = 8
    return pl.pallas_call(
        functools.partial(count_kernel, group),
        out_shape=jax.ShapeDtypeStruct((size, size), BF),
        in_specs=[
            pl.BlockSpec(memory_space=pltpu.SMEM),
            pl.BlockSpec(memory_space=pltpu.SMEM),
            pl.BlockSpec(memory_space=pl.ANY),
        ],
        out_specs=pl.BlockSpec(memory_space=pltpu.VMEM),
        scratch_shapes=[
            pltpu.VMEM(mask.shape, jnp.int32),
            pltpu.SemaphoreType.DMA((tiles // group,)),
        ],
        name="count_edges",
    )(coord, count, mask)


def layers_kernel(
    number,
    slots,
    step,
    feat_hbm,
    a_hbm,
    enc_col,
    enc_row,
    ws1_hbm,
    wn1_hbm,
    b1,
    ws2_hbm,
    wn2_hbm,
    b2,
    out_hbm,
    table,
    a,
    ws1,
    wn1,
    ws2,
    wn2,
    pick,
    spread,
    acc,
    selfp,
    denom,
    live_m,
    outv,
    sent,
    came,
    sent_n,
    came_n,
    load_sem,
    out_sem,
    send_sem,
    recv_sem,
    own_sem,
    n_sem,
):
    me = lax.axis_index("vert")
    rows, width = feat_hbm.shape
    mir = number * slots
    kb = width // LANES
    chunk = slots * kb
    flat = mir * kb
    size = rows + mir

    barrier = pltpu.get_barrier_semaphore()

    @pl.loop(1, number)
    def _(s):
        pl.semaphore_signal(barrier, inc=1, device_id=(lax.rem(me + s, number),), device_id_type=pl.DeviceIdType.MESH)

    loads = [
        pltpu.make_async_copy(feat_hbm, table.at[pl.ds(0, rows)], load_sem.at[0]),
        pltpu.make_async_copy(a_hbm, a, load_sem.at[1]),
        pltpu.make_async_copy(ws1_hbm, ws1, load_sem.at[2]),
        pltpu.make_async_copy(wn1_hbm, wn1, load_sem.at[3]),
        pltpu.make_async_copy(ws2_hbm, ws2, load_sem.at[4]),
        pltpu.make_async_copy(wn2_hbm, wn2, load_sem.at[5]),
    ]
    for load in loads:
        load.start()

    def iota(shape, dim):
        return lax.broadcasted_iota(jnp.int32, shape, dim)

    def one_hot(cond):
        return jnp.where(cond, 1.0, 0.0).astype(BF)

    pick[...] = one_hot(iota((mir, rows), 1) == enc_col[...])
    live_s = enc_col[...] >= 0
    spread[...] = one_hot(iota((rows, mir), 0) == enc_row[...])
    fr = iota((flat, mir), 0)
    to_flat = one_hot((fr // chunk) * slots + fr % slots == iota((flat, mir), 1))
    fc = iota((mir, flat), 1)
    from_flat = one_hot((fc // chunk) * slots + fc % slots == iota((mir, flat), 0))
    part = (iota((flat, LANES), 0) % chunk) // slots

    def pack(phase, value):
        wide = mm(to_flat, value)
        total = jnp.zeros((flat, LANES), F32)
        for k in range(kb):
            total = jnp.where(part == k, wide[:, k * LANES : (k + 1) * LANES], total)
        sent[phase] = total.astype(BF)

    def unpack(phase):
        narrow = came[phase]
        zero = jnp.zeros_like(narrow)
        wide = jnp.concatenate([jnp.where(part == k, narrow, zero) for k in range(kb)], axis=1)
        return mm(from_flat, wide)

    def send(phase):
        pltpu.make_async_copy(
            sent.at[phase, pl.ds(me * chunk, chunk)], came.at[phase, pl.ds(me * chunk, chunk)], own_sem.at[phase]
        ).start()

        @pl.loop(1, number)
        def _(s):
            dst = lax.rem(me + s, number)
            pltpu.make_async_remote_copy(
                src_ref=sent.at[phase, pl.ds(dst * chunk, chunk)],
                dst_ref=came.at[phase, pl.ds(me * chunk, chunk)],
                send_sem=send_sem.at[phase],
                recv_sem=recv_sem.at[phase],
                device_id=(dst,),
                device_id_type=pl.DeviceIdType.MESH,
            ).start()

    def wait_bytes(ref, sem):
        pltpu.make_async_copy(ref, ref, sem).wait()

    others = pl.ds(0, (number - 1) * chunk)

    def arrive(phase):
        pltpu.make_async_copy(
            sent.at[phase, pl.ds(me * chunk, chunk)], came.at[phase, pl.ds(me * chunk, chunk)], own_sem.at[phase]
        ).wait()
        wait_bytes(came.at[phase, others], recv_sem.at[phase])

    blocks = rows // step

    def over_rows(fn):
        @pl.loop(0, blocks)
        def _(b):
            fn(pl.ds(pl.multiple_of(b * step, step), step))

    loads[0].wait()
    gathered = mm(pick[...], table[pl.ds(0, rows), :])
    feat_s = gathered.astype(BF)
    pack(0, jnp.where(live_s, gathered, DEAD).astype(BF))
    pl.semaphore_wait(barrier, number - 1)
    send(0)

    loads[2].wait()

    def self1(span):
        selfp[span, :] = mm(table[span, :], ws1[...]) + b1[...].astype(F32)

    over_rows(self1)
    self_s = mm(feat_s, ws1[...]) + b1[...].astype(F32)
    same = mm(pick[...], spread[...]).astype(BF)
    loads[1].wait()
    a_s = mm(pick[...], a[pl.ds(0, rows), :]).astype(BF)

    arrive(0)
    got = unpack(0)
    alive = got[:, :1] < DEAD / 2
    live_m[...] = jnp.broadcast_to(one_hot(alive), (mir, LANES))
    table[pl.ds(rows, mir), :] = jnp.where(alive, got, 0.0).astype(BF)
    ones = jnp.concatenate([jnp.ones((rows, LANES), BF), live_m[...]], axis=0)

    a_m = a[pl.ds(rows, mir), :]
    diag = one_hot(iota((mir, size), 1) == iota((mir, size), 0) + rows)
    a_m = a_m - diag
    a[pl.ds(rows, mir), :] = a_m
    pack(1, mm(a_m, table[...]).astype(BF))
    send(1)
    counted = mm(a_m, ones)[:, :1]
    high = jnp.floor(counted * (1.0 / 256.0))
    low = counted - high * 256.0
    slot_of = iota((mir, mir), 0) % slots
    at_me = iota((mir, mir), 1) == me * slots + slot_of
    by_peer = one_hot(iota((number, mir), 1) // slots == iota((number, mir), 0))
    sent_n[:, 0, :] = mm(by_peer, jnp.where(at_me, high, 0.0).astype(BF)) * 256.0 + mm(
        by_peer, jnp.where(at_me, low, 0.0).astype(BF)
    )
    own_n = pltpu.make_async_copy(sent_n.at[me], came_n.at[me], n_sem.at[0])
    own_n.start()

    @pl.loop(1, number)
    def _(s):
        dst = lax.rem(me + s, number)
        pltpu.make_async_remote_copy(
            src_ref=sent_n.at[dst],
            dst_ref=came_n.at[me],
            send_sem=n_sem.at[1],
            recv_sem=n_sem.at[2],
            device_id=(dst,),
            device_id_type=pl.DeviceIdType.MESH,
        ).start()

    acc_s = mm(a_s, table[...])
    denom_s = mm(a_s, ones)[:, :1]

    def own1(span):
        acc[span, :] = mm(a[span, :], table[...])
        denom[span, :] = mm(a[span, :], ones)

    over_rows(own1)
    loads[3].wait()

    own_n.wait()
    wait_bytes(came_n.at[pl.ds(0, number - 1)], n_sem.at[2])
    counts = jnp.sum(came_n[:, 0, :], axis=0, keepdims=True)
    denom_s = denom_s + jnp.sum(same.astype(F32) * counts, axis=1, keepdims=True)

    arrive(1)
    ret = unpack(1).astype(BF)
    mean_s = ((acc_s + mm(same, ret)) / jnp.maximum(denom_s, 1.0)).astype(BF)
    hid_s = jnp.maximum(self_s + mm(mean_s, wn1[...]), 0.0).astype(BF)
    pack(2, hid_s)
    send(2)

    def hidden(span):
        full = denom[span, :1] + jnp.sum(spread[span, :].astype(F32) * counts, axis=1, keepdims=True)
        denom[span, :] = jnp.broadcast_to(full, (step, LANES))
        mean = ((acc[span, :] + mm(spread[span, :], ret)) / full).astype(BF)
        table[span, :] = jnp.maximum(selfp[span, :] + mm(mean, wn1[...]), 0.0).astype(BF)

    over_rows(hidden)
    partial = mm(a[pl.ds(rows, mir), pl.ds(0, rows)], table[pl.ds(0, rows), :])
    loads[4].wait()

    def self2(span):
        selfp[span, :] = mm(table[span, :], ws2[...]) + b2[...].astype(F32)

    over_rows(self2)

    def own2(span):
        acc[span, :] = mm(a[span, pl.ds(0, rows)], table[pl.ds(0, rows), :])

    over_rows(own2)
    loads[5].wait()

    arrive(2)
    second = (unpack(2) * live_m[:, :1].astype(F32)).astype(BF)
    table[pl.ds(rows, mir), :] = second
    pack(3, (partial + mm(a[pl.ds(rows, mir), pl.ds(rows, mir)], second)).astype(BF))
    send(3)

    def more2(span):
        acc[span, :] += mm(a[span, pl.ds(rows, mir)], table[pl.ds(rows, mir), :])

    over_rows(more2)
    arrive(3)
    ret2 = unpack(3).astype(BF)

    def last(span):
        mean = ((acc[span, :] + mm(spread[span, :], ret2)) / denom[span, :1]).astype(BF)
        outv[span, :] = (selfp[span, :] + mm(mean, wn2[...])).astype(BF)

    over_rows(last)
    flush = pltpu.make_async_copy(outv, out_hbm, out_sem)
    flush.start()
    for phase in range(4):
        wait_bytes(sent.at[phase, others], send_sem.at[phase])
    wait_bytes(sent_n.at[pl.ds(0, number - 1)], n_sem.at[1])
    flush.wait()


def run_layers(number, slots, features, a, enc, w_self1, w_neigh1, bias1, w_self2, w_neigh2, bias2):
    rows, width = features.shape
    mir = number * slots
    size = rows + mir
    flat = mir * (width // LANES)
    any_spec = pl.BlockSpec(memory_space=pl.ANY)
    vm = pl.BlockSpec(memory_space=pltpu.VMEM)
    step = 256
    return pl.pallas_call(
        functools.partial(layers_kernel, number, slots, step),
        out_shape=jax.ShapeDtypeStruct((rows, width), BF),
        in_specs=[any_spec, any_spec, vm, vm, any_spec, any_spec, vm, any_spec, any_spec, vm],
        out_specs=any_spec,
        scratch_shapes=[
            pltpu.VMEM((size, width), BF),
            pltpu.VMEM((size, size), BF),
            pltpu.VMEM((width, width), BF),
            pltpu.VMEM((width, width), BF),
            pltpu.VMEM((width, width), BF),
            pltpu.VMEM((width, width), BF),
            pltpu.VMEM((mir, rows), BF),
            pltpu.VMEM((rows, mir), BF),
            pltpu.VMEM((rows, width), F32),
            pltpu.VMEM((rows, width), F32),
            pltpu.VMEM((rows, LANES), F32),
            pltpu.VMEM((mir, LANES), BF),
            pltpu.VMEM((rows, width), BF),
            pltpu.VMEM((4, flat, LANES), BF),
            pltpu.VMEM((4, flat, LANES), BF),
            pltpu.VMEM((number, 1, mir), F32),
            pltpu.VMEM((number, 1, mir), F32),
            pltpu.SemaphoreType.DMA((6,)),
            pltpu.SemaphoreType.DMA,
            pltpu.SemaphoreType.DMA((4,)),
            pltpu.SemaphoreType.DMA((4,)),
            pltpu.SemaphoreType.DMA((4,)),
            pltpu.SemaphoreType.DMA((3,)),
        ],
        compiler_params=pltpu.CompilerParams(
            collective_id=0, has_side_effects=True, vmem_limit_bytes=60 * 1024 * 1024
        ),
        name="layers",
    )(
        features,
        a,
        enc.reshape(mir, 1),
        enc.reshape(1, mir),
        w_self1,
        w_neigh1,
        bias1.reshape(1, width),
        w_self2,
        w_neigh2,
        bias2.reshape(1, width),
    )


def body(
    features,
    send_rows,
    mirror_count,
    tile_coord,
    tile_mask,
    tile_count,
    w_self1,
    w_neigh1,
    bias1,
    w_self2,
    w_neigh2,
    bias2,
):
    number = lax.axis_size("vert")
    rows, _ = features.shape
    slots = send_rows.shape[2]
    live = jnp.arange(slots, dtype=jnp.int32)[None, :] < mirror_count[0][:, None]
    enc = jnp.where(live, send_rows[0], -1)
    a = count_edges(tile_coord[0], tile_count, tile_mask[0], rows + number * slots)
    return run_layers(number, slots, features, a, enc, w_self1, w_neigh1, bias1, w_self2, w_neigh2, bias2)


def solution(mesh):
    in_specs = (
        P("vert", None),
        P("vert", None, None),
        P("vert", None),
        P("vert", None, None),
        P("vert", None, None, None),
        P("vert"),
        P(),
        P(),
        P(),
        P(),
        P(),
        P(),
    )
    out_specs = P("vert", None)
    return jax.shard_map(body, mesh=mesh, in_specs=in_specs, out_specs=out_specs, check_vma=False)
```

time: 307 us -> 50.2 us (0.16)
  starting transfers between devices: 126 us -> 0 us
  other arithmetic: 73.8 us -> 1.96 us
  Pallas kernels: 0 us -> 41.4 us
  matrix products: 40.1 us -> 0 us
  waiting for transfers between devices: 33.2 us -> 0 us
  local copies, waits for them, and re-layouts: 30.3 us -> 5.91 us
    all_to_all x6 -> x0, starting transfers between devices: 126 us -> none  [mirror_route(): lax.all_to_all(for_sending(parts), 'vert', split_axis=0, concat_axis=0, t...]
    scatter-add x9 -> x0, other arithmetic: 56.4 us -> none  [the longest x4 47.1 us: visit(): totals = totals.at[target].add(products)]
    pallas_call x0 -> x2, Pallas kernels: none -> 41.4 us  [the longest x1 35.7 us: run_layers(): pl.pallas_call(functools.partial(layers_kernel, number, slots, step), out...]
    dot_general x8 -> x0, matrix products: 40.1 us -> none  [the longest x4 29.4 us: visit(): jnp.einsum('tij,tjf->tif', weights, jnp.take(table_blocks, source, axis=0...]
    all_to_all x6 -> x0, waiting for transfers between devices: 33.2 us -> none  [mirror_route(): lax.all_to_all(for_sending(parts), 'vert', split_axis=0, concat_axis=0, t...]
    gather x10 -> x0, local copies, waits for them, and re-layouts: 21.7 us -> none  [the longest x4 16.2 us: visit(): jnp.take(table_blocks, source, axis=0)]
    reduce_sum x2 -> x0, other arithmetic: 4.55 us -> none  [visit(): degree = degree.at[target].add(jnp.sum(weights.astype(jnp.float32), axis=2))]
    another operation x3 -> x0, other arithmetic: 3.85 us -> none
  transfers between devices with their start and end apart: 6 -> 0, of which waited for: 5 -> 0; matrix products, arithmetic and copies ran while one was open for 5% -> 0% of each run, Pallas kernels for 0% -> 0%
where the time goes in v1:
time: 50.2 us; the launch traced here: 50 us
  Pallas kernels  41.4 us (82%)
  local copies, waits for them, and re-layouts  5.91 us (12%)
  other arithmetic  1.96 us (4%)
  between operations  0.68 us (1%)
    pallas_call x1, Pallas kernels, run_layers(): pl.pallas_call(functools.partial(layers_kernel, number, slots, step), out...  35.7 us
    pallas_call x1, Pallas kernels, count_edges(): pl.pallas_call(functools.partial(count_kernel, group), out_shape=jax.Shap...  5.68 us
    unnamed x2, local copies, waits for them, and re-layouts  3.03 us
    reshape x1, local copies, waits for them, and re-layouts, run_layers(): bias1.reshape(1, width)  1.26 us
    reshape x1, local copies, waits for them, and re-layouts, run_layers(): bias2.reshape(1, width)  1.25 us
    select_n x2, other arithmetic, body(): enc = jnp.where(live, send_rows[0], -1)  1.23 us

profile of v1, /device:TPU:0, one launch (start us, length us, event | category | flops | bytes accessed | tf_op | source)
XLA Modules:
  0.0 50.0 jit_solution(2663271409624344280)
XLA Ops:
  0.7 1.3 %reshape.73.b1 = bf16[1,512]{1,0:T(2,128)(2,1)} reshape(bf16[512]{0:T(512)(128)(2,1)} %param.20) | data formatting | bytes 2048 | tf_op jit(solution)/shard_map/reshape | solution.py:377
  1.9 1.2 %reshape.74.b2 = bf16[1,512]{1,0:T(2,128)(2,1)} reshape(bf16[512]{0:T(512)(128)(2,1)} %param.23) | data formatting | bytes 2048 | tf_op jit(solution)/shard_map/reshape | solution.py:380
  3.2 0.7 %iota_compare_fusion = pred[32,4]{1,0:T(8,128)(4,1)S(1)} fusion(s32[32]{0:T(128)} %bitcast.5), kind=kLoop, calls=%fused_computation.1 | loop fusion | flops 128 | bytes 256 | tf_op jit(solution)/shard_map/lt | solution.py:401
  3.9 0.1 lt.40
  4.0 0.1 lt.41
  4.1 0.8 %copy.17 = s32[1,32,4]{2,1,0:T(8,128)S(1)} copy(s32[1,32,4]{1,2,0:T(4,128)} %param.13) | data formatting | bytes 1024 | tf_op args[1]
  4.9 0.1 squeeze.14
  5.0 0.6 %broadcast_select_fusion.1.enc_row = s32[1,128]{1,0:T(1,128)} fusion(pred[1,128]{1,0:T(4,128)(4,1)S(1)} %lt.40, s32[1,128]{1,0:T(1,128)S(1)} %squeeze.14), kind=kLoop, calls=%fused_computation.2 | loop fusion | flops 128 | bytes 1152 | tf_op jit(solution)/shard_map/jit(_where)/select_n | solution.py:402
  5.6 0.1 squeeze.15
  5.6 0.6 %broadcast_select_fusion.enc_col = s32[128,1]{1,0:T(8,128)} fusion(pred[128,1]{1,0:T(8,128)(4,1)S(1)} %lt.41, s32[128,1]{1,0:T(8,128)S(1)} %squeeze.15), kind=kLoop, calls=%fused_computation | loop fusion | flops 128 | bytes 1152 | tf_op jit(solution)/shard_map/jit(_where)/select_n | solution.py:402
  6.3 5.7 %count_edges.1.a_hbm = bf16[1152,1152]{1,0:T(8,128)(2,1)} custom-call(s32[2,128]{1,0:T(2,128)} %bitcast.4, s32[1]{0:T(128)S(6)} %copy.22.count, s32[128,128,128]{2,1,0:T(8,128)} %bitcast.3), custom_call_target="tpu_custom_call" | custom-call | tf_op jit(solution)/shard_map/count_edges/pallas_call | solution.py:60
  12.0 35.7 %layers.1 = bf16[1024,512]{1,0:T(8,128)(2,1)} custom-call(bf16[1024,512]{1,0:T(8,128)(2,1)} %feat_hbm.1, bf16[1152,1152]{1,0:T(8,128)(2,1)} %count_edges.1.a_hbm, s32[128,1]{1,0:T(8,128)} %broadcast_select_fusion.enc_col, s32[1,128]{1,0:T(1,128)} %broadcast_select_fusion.1.enc_row, bf16[512,512]{1,0:T(8,128)(2,1)} %ws1_hbm.1, bf16[512,512]{1,0:T(8,128)(2,1)} %wn1_hbm.1, ...), custom_call_target="tpu_custom_call" | custom-call | tf_op jit(solution)/shard_map/layers/pallas_call | solution.py:336
  47.7 2.3 %copy.23 = bf16[1024,512]{1,0:T(8,128)(2,1)} copy(bf16[1024,512]{1,0:T(8,128)(2,1)} %layers.1) | data formatting | bytes 2097152

commit v2 on v1

--- a/solution.py
+++ b/solution.py
@@ -17,71 +17,16 @@
     return jnp.dot(a, b, preferred_element_type=F32)
 
 
-def count_kernel(group, coord, count, mask, out, held, sems):
-    tiles, block, _ = mask.shape
-    size = out.shape[0]
-    live = count[0]
-    groups = tiles // group
-
-    def copy(g):
-        span = pl.ds(g * group, group)
-        return pltpu.make_async_copy(mask.at[span], held.at[span], sems.at[g])
-
-    for g in range(groups):
-
-        @pl.when(g * group < live)
-        def _():
-            copy(g).start()
-
-    step = block
-
-    @pl.loop(0, size // step)
-    def _(b):
-        rows = lax.broadcasted_iota(jnp.int32, (step, size), 0) + b * step
-        cols = lax.broadcasted_iota(jnp.int32, (step, size), 1)
-        out[pl.ds(pl.multiple_of(b * step, step), step), :] = jnp.where(rows == cols, 1.0, 0.0).astype(BF)
-
-    for g in range(groups):
-
-        @pl.when(g * group < live)
-        def _():
-            copy(g).wait()
-
-            @pl.loop(g * group, jnp.minimum((g + 1) * group, live))
-            def _(t):
-                rows = pl.ds(pl.multiple_of(coord[0, t] * block, block), block)
-                cols = pl.ds(pl.multiple_of(coord[1, t] * block, block), block)
-                out[rows, cols] += held[t].astype(F32).astype(BF)
-
-
-def count_edges(coord, count, mask, size):
-    tiles, block, _ = mask.shape
-    group = 8
-    return pl.pallas_call(
-        functools.partial(count_kernel, group),
-        out_shape=jax.ShapeDtypeStruct((size, size), BF),
-        in_specs=[
-            pl.BlockSpec(memory_space=pltpu.SMEM),
-            pl.BlockSpec(memory_space=pltpu.SMEM),
-            pl.BlockSpec(memory_space=pl.ANY),
-        ],
-        out_specs=pl.BlockSpec(memory_space=pltpu.VMEM),
-        scratch_shapes=[
-            pltpu.VMEM(mask.shape, jnp.int32),
-            pltpu.SemaphoreType.DMA((tiles // group,)),
-        ],
-        name="count_edges",
-    )(coord, count, mask)
-
-
 def layers_kernel(
     number,
     slots,
     step,
     feat_hbm,
-    a_hbm,
-    enc_col,
-    enc_row,
+    send_rows,
+    mirror_count,
+    coord,
+    mask_hbm,
+    tile_count,
     ws1_hbm,
     wn1_hbm,
     b1,
@@ -91,6 +36,10 @@
     out_hbm,
     table,
     a,
+    held,
+    prefix,
+    links,
+    link_s,
     ws1,
     wn1,
     ws2,
@@ -107,6 +56,8 @@
     sent_n,
     came_n,
     load_sem,
+    mask_sem,
+    link_sem,
     out_sem,
     send_sem,
     recv_sem,
@@ -129,13 +80,24 @@
 
     loads = [
         pltpu.make_async_copy(feat_hbm, table.at[pl.ds(0, rows)], load_sem.at[0]),
-        pltpu.make_async_copy(a_hbm, a, load_sem.at[1]),
-        pltpu.make_async_copy(ws1_hbm, ws1, load_sem.at[2]),
-        pltpu.make_async_copy(wn1_hbm, wn1, load_sem.at[3]),
-        pltpu.make_async_copy(ws2_hbm, ws2, load_sem.at[4]),
-        pltpu.make_async_copy(wn2_hbm, wn2, load_sem.at[5]),
+        pltpu.make_async_copy(ws1_hbm, ws1, load_sem.at[1]),
+        pltpu.make_async_copy(wn1_hbm, wn1, load_sem.at[2]),
+        pltpu.make_async_copy(ws2_hbm, ws2, load_sem.at[3]),
+        pltpu.make_async_copy(wn2_hbm, wn2, load_sem.at[4]),
     ]
-    for load in loads:
+    tiles, block = mask_hbm.shape[1], mask_hbm.shape[2]
+    groups = mask_sem.shape[0]
+    group = tiles // groups
+    blocks_a = size // block
+
+    def mask_copy(g):
+        span = pl.ds(g * group, group)
+        return pltpu.make_async_copy(mask_hbm.at[0, span], held.at[span], mask_sem.at[g])
+
+    loads[0].start()
+    for g in range(groups):
+        mask_copy(g).start()
+    for load in loads[1:]:
         load.start()
 
     def iota(shape, dim):
@@ -144,9 +106,37 @@
     def one_hot(cond):
         return jnp.where(cond, 1.0, 0.0).astype(BF)
 
-    pick[...] = one_hot(iota((mir, rows), 1) == enc_col[...])
-    live_s = enc_col[...] >= 0
-    spread[...] = one_hot(iota((rows, mir), 0) == enc_row[...])
+    def column_to_row(col, height):
+        return jnp.transpose(jnp.broadcast_to(col, (col.shape[0], height)))[:1, :]
+
+    key_row = (coord[0, :1, :] * blocks_a + coord[0, 1:2, :]).astype(F32)
+    key_col = jnp.transpose(jnp.broadcast_to(key_row, (LANES, tiles)))[:, :1].astype(jnp.int32)
+    key_row = key_row.astype(jnp.int32)
+    place = iota((tiles, tiles), 0)
+    before = jnp.where((key_col == key_row) & (place < iota((tiles, tiles), 1)), place + 1, 0)
+    wide_links = links.shape[1]
+    links[...] = jnp.zeros_like(links)
+    links[0:1, pl.ds(0, tiles)] = jnp.max(before, axis=0, keepdims=True)
+    spot = iota((tiles, wide_links), 0)
+    ended = (key_col == iota((tiles, wide_links), 1)) & (spot < tile_count[0])
+    links[1:2, :] = jnp.max(jnp.where(ended, spot + 1, 0), axis=0, keepdims=True)
+    to_scalar = pltpu.make_async_copy(links, link_s, link_sem)
+    to_scalar.start()
+
+    slot_col = iota((mir, 1), 0) % slots
+    expand = one_hot(slot_col == iota((mir, slots), 1))
+    raw = send_rows[0]
+    each = mm(expand, (raw // 256).astype(F32).astype(BF)) * 256.0 + mm(expand, (raw % 256).astype(F32).astype(BF))
+    peer_hit = iota((mir, number), 1) == iota((mir, number), 0) // slots
+    row_col = jnp.sum(jnp.where(peer_hit, each, 0.0), axis=1, keepdims=True)
+    count_col = jnp.sum(jnp.where(peer_hit, mirror_count[...], 0).astype(F32), axis=1, keepdims=True)
+    enc_f = jnp.where(slot_col.astype(F32) < count_col, row_col, -1.0)
+    enc_col = enc_f.astype(jnp.int32)
+    enc_row = column_to_row(enc_f, LANES).astype(jnp.int32)
+
+    pick[...] = one_hot(iota((mir, rows), 1) == enc_col)
+    live_s = enc_col >= 0
+    spread[...] = one_hot(iota((rows, mir), 0) == enc_row)
     fr = iota((flat, mir), 0)
     to_flat = one_hot((fr // chunk) * slots + fr % slots == iota((flat, mir), 1))
     fc = iota((mir, flat), 1)
@@ -208,15 +198,31 @@
     pl.semaphore_wait(barrier, number - 1)
     send(0)
 
-    loads[2].wait()
+    to_scalar.wait()
+    prefix[0] = jnp.zeros((block, block), BF)
+    for g in range(groups):
+        mask_copy(g).wait()
+
+        @pl.loop(g * group, (g + 1) * group, unroll=4)
+        def _(t):
+            prefix[t + 1] = held[t].astype(F32).astype(BF) + prefix[link_s[0, t]]
+
+    eye = one_hot(iota((block, block), 0) == iota((block, block), 1))
+    for b in range(blocks_a):
+        for c in range(blocks_a):
+            piece = prefix[link_s[1, b * blocks_a + c]]
+            if b == c and b < rows // block:
+                piece = piece + eye
+            a[b * block : (b + 1) * block, c * block : (c + 1) * block] = piece
+
+    loads[1].wait()
 
     def self1(span):
-        selfp[span, :] = mm(table[span, :], ws1[...]) + b1[...].astype(F32)
+        selfp[span, :] = mm(table[span, :], ws1[...]) + b1[...].astype(F32)[None, :]
 
     over_rows(self1)
-    self_s = mm(feat_s, ws1[...]) + b1[...].astype(F32)
+    self_s = mm(feat_s, ws1[...]) + b1[...].astype(F32)[None, :]
     same = mm(pick[...], spread[...]).astype(BF)
-    loads[1].wait()
     a_s = mm(pick[...], a[pl.ds(0, rows), :]).astype(BF)
 
     arrive(0)
@@ -227,9 +233,6 @@
     ones = jnp.concatenate([jnp.ones((rows, LANES), BF), live_m[...]], axis=0)
 
     a_m = a[pl.ds(rows, mir), :]
-    diag = one_hot(iota((mir, size), 1) == iota((mir, size), 0) + rows)
-    a_m = a_m - diag
-    a[pl.ds(rows, mir), :] = a_m
     pack(1, mm(a_m, table[...]).astype(BF))
     send(1)
     counted = mm(a_m, ones)[:, :1]
@@ -264,7 +267,7 @@
         denom[span, :] = mm(a[span, :], ones)
 
     over_rows(own1)
-    loads[3].wait()
+    loads[2].wait()
 
     own_n.wait()
     wait_bytes(came_n.at[pl.ds(0, number - 1)], n_sem.at[2])
@@ -286,10 +289,10 @@
 
     over_rows(hidden)
     partial = mm(a[pl.ds(rows, mir), pl.ds(0, rows)], table[pl.ds(0, rows), :])
-    loads[4].wait()
+    loads[3].wait()
 
     def self2(span):
-        selfp[span, :] = mm(table[span, :], ws2[...]) + b2[...].astype(F32)
+        selfp[span, :] = mm(table[span, :], ws2[...]) + b2[...].astype(F32)[None, :]
 
     over_rows(self2)
 
@@ -297,7 +300,7 @@
         acc[span, :] = mm(a[span, pl.ds(0, rows)], table[pl.ds(0, rows), :])
 
     over_rows(own2)
-    loads[5].wait()
+    loads[4].wait()
 
     arrive(2)
     second = (unpack(2) * live_m[:, :1].astype(F32)).astype(BF)
@@ -325,22 +328,45 @@
     flush.wait()
 
 
-def run_layers(number, slots, features, a, enc, w_self1, w_neigh1, bias1, w_self2, w_neigh2, bias2):
+def body(
+    features,
+    send_rows,
+    mirror_count,
+    tile_coord,
+    tile_mask,
+    tile_count,
+    w_self1,
+    w_neigh1,
+    bias1,
+    w_self2,
+    w_neigh2,
+    bias2,
+):
+    number = lax.axis_size("vert")
     rows, width = features.shape
+    slots = send_rows.shape[2]
+    _, tiles, block, _ = tile_mask.shape
     mir = number * slots
     size = rows + mir
     flat = mir * (width // LANES)
+    pairs = (size // block) ** 2
+    wide_links = -(-max(pairs, tiles) // LANES) * LANES
     any_spec = pl.BlockSpec(memory_space=pl.ANY)
     vm = pl.BlockSpec(memory_space=pltpu.VMEM)
+    sm = pl.BlockSpec(memory_space=pltpu.SMEM)
     step = 256
     return pl.pallas_call(
         functools.partial(layers_kernel, number, slots, step),
         out_shape=jax.ShapeDtypeStruct((rows, width), BF),
-        in_specs=[any_spec, any_spec, vm, vm, any_spec, any_spec, vm, any_spec, any_spec, vm],
+        in_specs=[any_spec, vm, vm, vm, any_spec, sm, any_spec, any_spec, vm, any_spec, any_spec, vm],
         out_specs=any_spec,
         scratch_shapes=[
             pltpu.VMEM((size, width), BF),
             pltpu.VMEM((size, size), BF),
+            pltpu.VMEM((tiles, block, block), jnp.int32),
+            pltpu.VMEM((tiles + 1, block, block), BF),
+            pltpu.VMEM((8, wide_links), jnp.int32),
+            pltpu.SMEM((8, wide_links), jnp.int32),
             pltpu.VMEM((width, width), BF),
             pltpu.VMEM((width, width), BF),
             pltpu.VMEM((width, width), BF),
@@ -356,7 +382,9 @@
             pltpu.VMEM((4, flat, LANES), BF),
             pltpu.VMEM((number, 1, mir), F32),
             pltpu.VMEM((number, 1, mir), F32),
-            pltpu.SemaphoreType.DMA((6,)),
+            pltpu.SemaphoreType.DMA((5,)),
+            pltpu.SemaphoreType.DMA((8,)),
+            pltpu.SemaphoreType.DMA,
             pltpu.SemaphoreType.DMA,
             pltpu.SemaphoreType.DMA((4,)),
             pltpu.SemaphoreType.DMA((4,)),
@@ -369,39 +397,18 @@
         name="layers",
     )(
         features,
-        a,
-        enc.reshape(mir, 1),
-        enc.reshape(1, mir),
+        jnp.swapaxes(send_rows, 1, 2),
+        mirror_count,
+        tile_coord,
+        tile_mask,
+        tile_count,
         w_self1,
         w_neigh1,
-        bias1.reshape(1, width),
+        bias1,
         w_self2,
         w_neigh2,
-        bias2.reshape(1, width),
+        bias2,
     )
-
-
-def body(
-    features,
-    send_rows,
-    mirror_count,
-    tile_coord,
-    tile_mask,
-    tile_count,
-    w_self1,
-    w_neigh1,
-    bias1,
-    w_self2,
-    w_neigh2,
-    bias2,
-):
-    number = lax.axis_size("vert")
-    rows, _ = features.shape
-    slots = send_rows.shape[2]
-    live = jnp.arange(slots, dtype=jnp.int32)[None, :] < mirror_count[0][:, None]
-    enc = jnp.where(live, send_rows[0], -1)
-    a = count_edges(tile_coord[0], tile_count, tile_mask[0], rows + number * slots)
-    return run_layers(number, slots, features, a, enc, w_self1, w_neigh1, bias1, w_self2, w_neigh2, bias2)
 
 
 def solution(mesh):

time: 50.2 us -> 38.9 us (0.77)
  Pallas kernels: 41.4 us -> 35.8 us
  local copies, waits for them, and re-layouts: 5.91 us -> 2.26 us
  other arithmetic: 1.96 us -> 0 us
    pallas_call x2 -> x1, Pallas kernels: 41.4 us -> 35.8 us  [body(): pl.pallas_call(functools.partial(layers_kernel, number, slots, step), out...]
    reshape x2 -> x0, local copies, waits for them, and re-layouts: 2.51 us -> none  [the longest x1 1.26 us: run_layers(): bias1.reshape(1, width)]
    select_n x2 -> x0, other arithmetic: 1.23 us -> none  [body(): enc = jnp.where(live, send_rows[0], -1)]
    unnamed x2 -> x1, local copies, waits for them, and re-layouts: 3.03 us -> 2.26 us
    lt x1 -> x0, other arithmetic: 0.73 us -> none  [body(): jnp.arange(slots, dtype=jnp.int32)[None, :] < mirror_count[0][:, None]]
where the time goes in v2:
time: 38.9 us; the launch traced here: 38.7 us
  Pallas kernels  35.8 us (92%)
  local copies, waits for them, and re-layouts  2.26 us (6%)
  between operations  0.66 us (2%)
    pallas_call x1, Pallas kernels, body(): pl.pallas_call(functools.partial(layers_kernel, number, slots, step), out...  35.8 us
    unnamed x1, local copies, waits for them, and re-layouts  2.26 us

profile of v2, /device:TPU:0, one launch (start us, length us, event | category | flops | bytes accessed | tf_op | source)
XLA Modules:
  0.0 38.7 jit_solution(7431078354243511832)
XLA Ops:
  0.7 35.8 %layers.1 = bf16[1024,512]{1,0:T(8,128)(2,1)} custom-call(bf16[1024,512]{1,0:T(8,128)(2,1)} %feat_hbm.1, s32[1,4,32]{2,1,0:T(4,128)} %bitcast.1, s32[1,32]{1,0:T(1,128)} %mirror_count.1, s32[1,2,128]{2,1,0:T(2,128)} %coord.1, s32[1,128,128,128]{3,2,1,0:T(8,128)} %mask_hbm.1, s32[1]{0:T(128)S(6)} %copy.14.tile_count, bf16[512,512]{1,0:T(8,128)(2,1)} %ws1_hbm.1, ...), custom_call_target="tpu_custom_call" | custom-call | tf_op jit(solution)/shard_map/layers/pallas_call | solution.py:358
  36.4 2.3 %copy.15 = bf16[1024,512]{1,0:T(8,128)(2,1)} copy(bf16[1024,512]{1,0:T(8,128)(2,1)} %layers.1) | data formatting | bytes 2097152

commit v3 on v2

--- a/solution.py
+++ b/solution.py
@@ -11,6 +11,14 @@
 DEAD = 64.0
 BF = jnp.bfloat16
 F32 = jnp.float32
+
+
+def div(x, n):
+    return x >> (n.bit_length() - 1) if n & (n - 1) == 0 else x // n
+
+
+def mod(x, n):
+    return x & (n - 1) if n & (n - 1) == 0 else x % n
 
 
 def mm(a, b):
@@ -44,6 +52,9 @@
     wn1,
     ws2,
     wn2,
+    a_flat,
+    a_packed,
+    base,
     pick,
     spread,
     acc,
@@ -123,11 +134,11 @@
     to_scalar = pltpu.make_async_copy(links, link_s, link_sem)
     to_scalar.start()
 
-    slot_col = iota((mir, 1), 0) % slots
+    slot_col = mod(iota((mir, 1), 0), slots)
     expand = one_hot(slot_col == iota((mir, slots), 1))
     raw = send_rows[0]
-    each = mm(expand, (raw // 256).astype(F32).astype(BF)) * 256.0 + mm(expand, (raw % 256).astype(F32).astype(BF))
-    peer_hit = iota((mir, number), 1) == iota((mir, number), 0) // slots
+    each = mm(expand, (div(raw, 256)).astype(F32).astype(BF)) * 256.0 + mm(expand, (mod(raw, 256)).astype(F32).astype(BF))
+    peer_hit = iota((mir, number), 1) == div(iota((mir, number), 0), slots)
     row_col = jnp.sum(jnp.where(peer_hit, each, 0.0), axis=1, keepdims=True)
     count_col = jnp.sum(jnp.where(peer_hit, mirror_count[...], 0).astype(F32), axis=1, keepdims=True)
     enc_f = jnp.where(slot_col.astype(F32) < count_col, row_col, -1.0)
@@ -138,23 +149,27 @@
     live_s = enc_col >= 0
     spread[...] = one_hot(iota((rows, mir), 0) == enc_row)
     fr = iota((flat, mir), 0)
-    to_flat = one_hot((fr // chunk) * slots + fr % slots == iota((flat, mir), 1))
+    to_flat = one_hot(div(fr, chunk) * slots + mod(fr, slots) == iota((flat, mir), 1))
     fc = iota((mir, flat), 1)
-    from_flat = one_hot((fc // chunk) * slots + fc % slots == iota((mir, flat), 0))
-    part = (iota((flat, LANES), 0) % chunk) // slots
+    from_flat = one_hot(div(fc, chunk) * slots + mod(fc, slots) == iota((mir, flat), 0))
+    part = div(mod(iota((flat, LANES), 0), chunk), slots)
+
+    def own_lanes(wide):
+        total = wide[:, :LANES]
+        for k in range(1, kb):
+            total = jnp.where(part == k, wide[:, k * LANES : (k + 1) * LANES], total)
+        return total
 
     def pack(phase, value):
-        wide = mm(to_flat, value)
-        total = jnp.zeros((flat, LANES), F32)
-        for k in range(kb):
-            total = jnp.where(part == k, wide[:, k * LANES : (k + 1) * LANES], total)
-        sent[phase] = total.astype(BF)
-
-    def unpack(phase):
+        sent[phase] = own_lanes(mm(to_flat, value)).astype(BF)
+
+    def widen(phase):
         narrow = came[phase]
         zero = jnp.zeros_like(narrow)
-        wide = jnp.concatenate([jnp.where(part == k, narrow, zero) for k in range(kb)], axis=1)
-        return mm(from_flat, wide)
+        return jnp.concatenate([jnp.where(part == k, narrow, zero) for k in range(kb)], axis=1)
+
+    def unpack(phase):
+        return mm(from_flat, widen(phase))
 
     def send(phase):
         pltpu.make_async_copy(
@@ -215,34 +230,36 @@
                 piece = piece + eye
             a[b * block : (b + 1) * block, c * block : (c + 1) * block] = piece
 
-    loads[1].wait()
-
-    def self1(span):
-        selfp[span, :] = mm(table[span, :], ws1[...]) + b1[...].astype(F32)[None, :]
-
-    over_rows(self1)
-    self_s = mm(feat_s, ws1[...]) + b1[...].astype(F32)[None, :]
-    same = mm(pick[...], spread[...]).astype(BF)
-    a_s = mm(pick[...], a[pl.ds(0, rows), :]).astype(BF)
+    a_flat[...] = mm(to_flat, a[pl.ds(rows, mir), pl.ds(0, rows)]).astype(BF)
+    base[...] = own_lanes(mm(a_flat[...], table[pl.ds(0, rows), :]))
+    a_rep = mm(to_flat, a[pl.ds(rows, mir), pl.ds(rows, mir)]).astype(BF)
+    high = flat // 4
+    for h in range(4):
+        kr = div(mod(iota((high, flat), 0) + h * high, chunk), slots)
+        kc = div(mod(iota((high, flat), 1), chunk), slots)
+        piece = mm(a_rep[h * high : (h + 1) * high], from_flat)
+        a_packed[h * high : (h + 1) * high, :] = jnp.where(kr == kc, piece, 0.0).astype(BF)
 
     arrive(0)
+    fresh = came[0].astype(F32)
+    clean = jnp.where(fresh < DEAD / 2, fresh, 0.0).astype(BF)
+    sent[1] = (base[...] + mm(a_packed[...], clean)).astype(BF)
+    send(1)
+
     got = unpack(0)
     alive = got[:, :1] < DEAD / 2
     live_m[...] = jnp.broadcast_to(one_hot(alive), (mir, LANES))
     table[pl.ds(rows, mir), :] = jnp.where(alive, got, 0.0).astype(BF)
     ones = jnp.concatenate([jnp.ones((rows, LANES), BF), live_m[...]], axis=0)
-
     a_m = a[pl.ds(rows, mir), :]
-    pack(1, mm(a_m, table[...]).astype(BF))
-    send(1)
     counted = mm(a_m, ones)[:, :1]
-    high = jnp.floor(counted * (1.0 / 256.0))
-    low = counted - high * 256.0
-    slot_of = iota((mir, mir), 0) % slots
+    upper = jnp.floor(counted * (1.0 / 256.0))
+    lower = counted - upper * 256.0
+    slot_of = mod(iota((mir, mir), 0), slots)
     at_me = iota((mir, mir), 1) == me * slots + slot_of
-    by_peer = one_hot(iota((number, mir), 1) // slots == iota((number, mir), 0))
-    sent_n[:, 0, :] = mm(by_peer, jnp.where(at_me, high, 0.0).astype(BF)) * 256.0 + mm(
-        by_peer, jnp.where(at_me, low, 0.0).astype(BF)
+    by_peer = one_hot(div(iota((number, mir), 1), slots) == iota((number, mir), 0))
+    sent_n[:, 0, :] = mm(by_peer, jnp.where(at_me, upper, 0.0).astype(BF)) * 256.0 + mm(
+        by_peer, jnp.where(at_me, lower, 0.0).astype(BF)
     )
     own_n = pltpu.make_async_copy(sent_n.at[me], came_n.at[me], n_sem.at[0])
     own_n.start()
@@ -259,10 +276,16 @@
             device_id_type=pl.DeviceIdType.MESH,
         ).start()
 
+    loads[1].wait()
+    self_s = mm(feat_s, ws1[...]) + b1[...].astype(F32)[None, :]
+    same = mm(pick[...], spread[...]).astype(BF)
+    same_flat = mm(same, from_flat).astype(BF)
+    a_s = mm(pick[...], a[pl.ds(0, rows), :]).astype(BF)
     acc_s = mm(a_s, table[...])
     denom_s = mm(a_s, ones)[:, :1]
 
     def own1(span):
+        selfp[span, :] = mm(table[span, :], ws1[...]) + b1[...].astype(F32)[None, :]
         acc[span, :] = mm(a[span, :], table[...])
         denom[span, :] = mm(a[span, :], ones)
 
@@ -275,11 +298,12 @@
     denom_s = denom_s + jnp.sum(same.astype(F32) * counts, axis=1, keepdims=True)
 
     arrive(1)
+    safe_s = jnp.maximum(denom_s, 1.0)
+    mean_s = ((acc_s + mm(same_flat, widen(1))) / safe_s).astype(BF)
+    hid_s = jnp.maximum(self_s + mm(mean_s, wn1[...]), 0.0)
+    pack(2, jnp.where(live_s, hid_s, 0.0).astype(BF))
+    send(2)
     ret = unpack(1).astype(BF)
-    mean_s = ((acc_s + mm(same, ret)) / jnp.maximum(denom_s, 1.0)).astype(BF)
-    hid_s = jnp.maximum(self_s + mm(mean_s, wn1[...]), 0.0).astype(BF)
-    pack(2, hid_s)
-    send(2)
 
     def hidden(span):
         full = denom[span, :1] + jnp.sum(spread[span, :].astype(F32) * counts, axis=1, keepdims=True)
@@ -288,7 +312,7 @@
         table[span, :] = jnp.maximum(selfp[span, :] + mm(mean, wn1[...]), 0.0).astype(BF)
 
     over_rows(hidden)
-    partial = mm(a[pl.ds(rows, mir), pl.ds(0, rows)], table[pl.ds(0, rows), :])
+    base[...] = own_lanes(mm(a_flat[...], table[pl.ds(0, rows), :]))
     loads[3].wait()
 
     def self2(span):
@@ -303,29 +327,41 @@
     loads[4].wait()
 
     arrive(2)
-    second = (unpack(2) * live_m[:, :1].astype(F32)).astype(BF)
-    table[pl.ds(rows, mir), :] = second
-    pack(3, (partial + mm(a[pl.ds(rows, mir), pl.ds(rows, mir)], second)).astype(BF))
+    sent[3] = (base[...] + mm(a_packed[...], came[2])).astype(BF)
     send(3)
-
-    def more2(span):
-        acc[span, :] += mm(a[span, pl.ds(rows, mir)], table[pl.ds(rows, mir), :])
-
-    over_rows(more2)
+    table[pl.ds(rows, mir), :] = unpack(2).astype(BF)
+
+    def early(span):
+        total = acc[span, :] + mm(a[span, pl.ds(rows, mir)], table[pl.ds(rows, mir), :])
+        mean = (total / denom[span, :1]).astype(BF)
+        outv[span, :] = (selfp[span, :] + mm(mean, wn2[...])).astype(BF)
+
+    over_rows(early)
+    acc_s2 = mm(a_s, table[...])
+    self_s2 = mm(hid_s.astype(BF), ws2[...]) + b2[...].astype(F32)[None, :]
+    earlier = iota((mir, mir), 0) < iota((mir, mir), 1)
+    again = jnp.max(jnp.where(earlier, same.astype(F32), 0.0), axis=0, keepdims=True)
+
+    def firsts(span):
+        spread[span, :] = jnp.where(again > 0.0, 0.0, spread[span, :].astype(F32)).astype(BF)
+
+    over_rows(firsts)
     arrive(3)
-    ret2 = unpack(3).astype(BF)
-
-    def last(span):
-        mean = ((acc[span, :] + mm(spread[span, :], ret2)) / denom[span, :1]).astype(BF)
-        outv[span, :] = (selfp[span, :] + mm(mean, wn2[...])).astype(BF)
-
-    over_rows(last)
-    flush = pltpu.make_async_copy(outv, out_hbm, out_sem)
-    flush.start()
+    mean_s2 = ((acc_s2 + mm(same_flat, widen(3))) / safe_s).astype(BF)
+    out_s = (self_s2 + mm(mean_s2, wn2[...])).astype(BF)
+    flushes = []
+    for b in range(blocks):
+        span = pl.ds(b * step, step)
+        hit = spread[span, :]
+        touched = jnp.sum(hit.astype(F32), axis=1, keepdims=True) > 0.0
+        outv[span, :] = jnp.where(touched, mm(hit, out_s), outv[span, :].astype(F32)).astype(BF)
+        flushes.append(pltpu.make_async_copy(outv.at[span], out_hbm.at[span], out_sem.at[b]))
+        flushes[-1].start()
     for phase in range(4):
         wait_bytes(sent.at[phase, others], send_sem.at[phase])
     wait_bytes(sent_n.at[pl.ds(0, number - 1)], n_sem.at[1])
-    flush.wait()
+    for flush in flushes:
+        flush.wait()
 
 
 def body(
@@ -371,6 +407,9 @@
             pltpu.VMEM((width, width), BF),
             pltpu.VMEM((width, width), BF),
             pltpu.VMEM((width, width), BF),
+            pltpu.VMEM((flat, rows), BF),
+            pltpu.VMEM((flat, flat), BF),
+            pltpu.VMEM((flat, LANES), F32),
             pltpu.VMEM((mir, rows), BF),
             pltpu.VMEM((rows, mir), BF),
             pltpu.VMEM((rows, width), F32),
@@ -385,14 +424,14 @@
             pltpu.SemaphoreType.DMA((5,)),
             pltpu.SemaphoreType.DMA((8,)),
             pltpu.SemaphoreType.DMA,
-            pltpu.SemaphoreType.DMA,
+            pltpu.SemaphoreType.DMA((rows // step,)),
             pltpu.SemaphoreType.DMA((4,)),
             pltpu.SemaphoreType.DMA((4,)),
             pltpu.SemaphoreType.DMA((4,)),
             pltpu.SemaphoreType.DMA((3,)),
         ],
         compiler_params=pltpu.CompilerParams(
-            collective_id=0, has_side_effects=True, vmem_limit_bytes=60 * 1024 * 1024
+            collective_id=0, has_side_effects=True, vmem_limit_bytes=63 * 1024 * 1024
         ),
         name="layers",
     )(

time: 38.9 us -> 36.8 us (0.946)
  Pallas kernels: 35.8 us -> 33.7 us
    pallas_call x1, Pallas kernels: 35.8 us -> 33.7 us  [body(): pl.pallas_call(functools.partial(layers_kernel, number, slots, step), out...]
where the time goes in v3:
time: 36.8 us; the launch traced here: 36.6 us
  Pallas kernels  33.7 us (92%)
  local copies, waits for them, and re-layouts  2.26 us (6%)
  between operations  0.66 us (2%)
    pallas_call x1, Pallas kernels, body(): pl.pallas_call(functools.partial(layers_kernel, number, slots, step), out...  33.7 us
    unnamed x1, local copies, waits for them, and re-layouts  2.26 us

profile of v3, /device:TPU:0, one launch (start us, length us, event | category | flops | bytes accessed | tf_op | source)
XLA Modules:
  0.0 36.6 jit_solution(9527648952059536380)
XLA Ops:
  0.7 33.7 %layers.1 = bf16[1024,512]{1,0:T(8,128)(2,1)} custom-call(bf16[1024,512]{1,0:T(8,128)(2,1)} %feat_hbm.1, s32[1,4,32]{2,1,0:T(4,128)} %bitcast.1, s32[1,32]{1,0:T(1,128)} %mirror_count.1, s32[1,2,128]{2,1,0:T(2,128)} %coord.1, s32[1,128,128,128]{3,2,1,0:T(8,128)} %mask_hbm.1, s32[1]{0:T(128)S(6)} %copy.14.tile_count, bf16[512,512]{1,0:T(8,128)(2,1)} %ws1_hbm.1, ...), custom_call_target="tpu_custom_call" | custom-call | tf_op jit(solution)/shard_map/layers/pallas_call | solution.py:394
  34.4 2.3 %copy.15 = bf16[1024,512]{1,0:T(8,128)(2,1)} copy(bf16[1024,512]{1,0:T(8,128)(2,1)} %layers.1) | data formatting | bytes 2097152

commit v4 on v3

--- a/solution.py
+++ b/solution.py
@@ -41,7 +41,9 @@
     ws2_hbm,
     wn2_hbm,
     b2,
-    out_hbm,
+    early_hbm,
+    late,
+    first_hbm,
     table,
     a,
     held,
@@ -346,22 +348,26 @@
         spread[span, :] = jnp.where(again > 0.0, 0.0, spread[span, :].astype(F32)).astype(BF)
 
     over_rows(firsts)
+    flushes = [
+        pltpu.make_async_copy(outv, early_hbm, out_sem.at[0]),
+        pltpu.make_async_copy(spread, first_hbm, out_sem.at[1]),
+    ]
+    for flush in flushes:
+        flush.start()
     arrive(3)
     mean_s2 = ((acc_s2 + mm(same_flat, widen(3))) / safe_s).astype(BF)
-    out_s = (self_s2 + mm(mean_s2, wn2[...])).astype(BF)
-    flushes = []
-    for b in range(blocks):
-        span = pl.ds(b * step, step)
-        hit = spread[span, :]
-        touched = jnp.sum(hit.astype(F32), axis=1, keepdims=True) > 0.0
-        outv[span, :] = jnp.where(touched, mm(hit, out_s), outv[span, :].astype(F32)).astype(BF)
-        flushes.append(pltpu.make_async_copy(outv.at[span], out_hbm.at[span], out_sem.at[b]))
-        flushes[-1].start()
+    late[...] = (self_s2 + mm(mean_s2, wn2[...])).astype(BF)
     for phase in range(4):
         wait_bytes(sent.at[phase, others], send_sem.at[phase])
     wait_bytes(sent_n.at[pl.ds(0, number - 1)], n_sem.at[1])
     for flush in flushes:
         flush.wait()
+
+
+def select_kernel(early, late, first, out):
+    hit = first[...]
+    touched = jnp.sum(hit.astype(F32), axis=1, keepdims=True) > 0.0
+    out[...] = jnp.where(touched, mm(hit, late[...]), early[...].astype(F32)).astype(BF)
 
 
 def body(
@@ -391,11 +397,15 @@
     vm = pl.BlockSpec(memory_space=pltpu.VMEM)
     sm = pl.BlockSpec(memory_space=pltpu.SMEM)
     step = 256
-    return pl.pallas_call(
+    early, late, first = pl.pallas_call(
         functools.partial(layers_kernel, number, slots, step),
-        out_shape=jax.ShapeDtypeStruct((rows, width), BF),
+        out_shape=(
+            jax.ShapeDtypeStruct((rows, width), BF),
+            jax.ShapeDtypeStruct((mir, width), BF),
+            jax.ShapeDtypeStruct((rows, mir), BF),
+        ),
         in_specs=[any_spec, vm, vm, vm, any_spec, sm, any_spec, any_spec, vm, any_spec, any_spec, vm],
-        out_specs=any_spec,
+        out_specs=(any_spec, vm, any_spec),
         scratch_shapes=[
             pltpu.VMEM((size, width), BF),
             pltpu.VMEM((size, size), BF),
@@ -424,7 +434,7 @@
             pltpu.SemaphoreType.DMA((5,)),
             pltpu.SemaphoreType.DMA((8,)),
             pltpu.SemaphoreType.DMA,
-            pltpu.SemaphoreType.DMA((rows // step,)),
+            pltpu.SemaphoreType.DMA((2,)),
             pltpu.SemaphoreType.DMA((4,)),
             pltpu.SemaphoreType.DMA((4,)),
             pltpu.SemaphoreType.DMA((4,)),
@@ -448,6 +458,20 @@
         w_neigh2,
         bias2,
     )
+    tall = rows // 2
+    return pl.pallas_call(
+        select_kernel,
+        grid=(rows // tall,),
+        out_shape=jax.ShapeDtypeStruct((rows, width), BF),
+        in_specs=[
+            pl.BlockSpec((tall, width), lambda b: (b, 0)),
+            pl.BlockSpec((mir, width), lambda b: (0, 0)),
+            pl.BlockSpec((tall, mir), lambda b: (b, 0)),
+        ],
+        out_specs=pl.BlockSpec((tall, width), lambda b: (b, 0)),
+        compiler_params=pltpu.CompilerParams(vmem_limit_bytes=62 * 1024 * 1024),
+        name="select",
+    )(early, late, first)
 
 
 def solution(mesh):

time: 36.8 us -> 36.6 us (level)
  local copies, waits for them, and re-layouts: 2.26 us -> 0 us
  Pallas kernels: 33.7 us -> 35.8 us
    pallas_call x0 -> x1, Pallas kernels: none -> 2.67 us  [body(): pl.pallas_call(select_kernel, grid=(rows // tall,), out_shape=jax.ShapeDt...]
    unnamed x1 -> x0, local copies, waits for them, and re-layouts: 2.26 us -> none
    pallas_call x1, Pallas kernels: 33.7 us -> 33.1 us  [body(): pl.pallas_call(functools.partial(layers_kernel, number, slots, step), out...]
where the time goes in v4:
time: 36.6 us; the launch traced here: 36.5 us
  Pallas kernels  35.8 us (98%)
  between operations  0.66 us (2%)
    pallas_call x1, Pallas kernels, body(): pl.pallas_call(functools.partial(layers_kernel, number, slots, step), out...  33.1 us
    pallas_call x1, Pallas kernels, body(): pl.pallas_call(select_kernel, grid=(rows // tall,), out_shape=jax.ShapeDt...  2.67 us

profile of v4, /device:TPU:0, one launch (start us, length us, event | category | flops | bytes accessed | tf_op | source)
XLA Modules:
  0.0 36.5 jit_solution(5631018045869740077)
XLA Ops:
  0.7 33.1 %layers.1 = (bf16[1024,512]{1,0:T(8,128)(2,1)}, bf16[128,512]{1,0:T(8,128)(2,1)}, bf16[1024,128]{1,0:T(8,128)(2,1)}) custom-call(bf16[1024,512]{1,0:T(8,128)(2,1)} %feat_hbm.1, s32[1,4,32]{2,1,0:T(4,128)} %bitcast.1, s32[1,32]{1,0:T(1,128)} %mirror_count.1, s32[1,2,128]{2,1,0:T(2,128)} %coord.1, s32[1,128,128,128]{3,2,1,0:T(8,128)} %mask_hbm.1, ...), custom_call_target="tpu_custom_call" | custom-call | tf_op jit(solution)/shard_map/layers/pallas_call | solution.py:400
  33.8 2.7 %select.1 = bf16[1024,512]{1,0:T(8,128)(2,1)} custom-call(bf16[1024,512]{1,0:T(8,128)(2,1)} %get-tuple-element.8.early, bf16[128,512]{1,0:T(8,128)(2,1)} %get-tuple-element.9.late, bf16[1024,128]{1,0:T(8,128)(2,1)} %get-tuple-element.10.first), custom_call_target="tpu_custom_call" | custom-call | tf_op jit(solution)/shard_map/select/pallas_call | solution.py:462
